TPU v7x, 32 devices: a whole 2x2x4 slice. The times are simulated.
32 devices in a mesh: dp: 8 (over z, y), tensor: 4 (over x, core).
Axes of the slice: x: 2, y: 2, z: 4, core: 2. Of those that a mesh axis runs over, the one named last changes fastest.
Arguments:
- tokens: bfloat16 [32768, 768], P(('dp', 'tensor')), may hold values from -6 to 6
- doc_lengths: int32 [32, 16], P('dp'), may hold values from 1 to 512, 1024 in all within a row
- w_query: bfloat16 [768, 768], P('dp', 'tensor'), may hold values from -0.21875 to 0.21875
- w_key: bfloat16 [768, 768], P('dp', 'tensor'), may hold values from -0.21875 to 0.21875
- w_value: bfloat16 [768, 768], P('dp', 'tensor'), may hold values from -0.21875 to 0.21875
- w_out: bfloat16 [768, 768], P('tensor', 'dp'), may hold values from -1.25 to 1.25
- w_up: bfloat16 [768, 3072], P('dp', 'tensor'), may hold values from -0.21875 to 0.21875
- w_down: bfloat16 [3072, 768], P('tensor', 'dp'), may hold values from -0.109375 to 0.109375
- b_query: bfloat16 [12, 64], P('tensor', 'dp'), may hold values from -3 to 3
- b_value: bfloat16 [12, 64], P('tensor', 'dp'), may hold values from -3 to 3
- b_up: bfloat16 [24, 128], P('tensor', 'dp'), may hold values from -3 to 3
- b_out: float32 [768], P(('dp', 'tensor')), may hold values from -3 to 3
- b_down: float32 [768], P(('dp', 'tensor')), may hold values from -3 to 3
- gain_one: float32 [768], P(('dp', 'tensor')), may hold values from 0.1 to 1.9
- shift_one: float32 [768], P(('dp', 'tensor')), may hold values from -3 to 3
- gain_two: float32 [768], P(('dp', 'tensor')), may hold values from 0.1 to 1.9
- shift_two: float32 [768], P(('dp', 'tensor')), may hold values from -3 to 3
- cotangent: bfloat16 [32768, 768], P(('dp', 'tensor')), may hold values from -6 to 6
Outputs:
- layer_out: bfloat16 [32768, 768], P(('dp', 'tensor'))
- grad_tokens: bfloat16 [32768, 768], P(('dp', 'tensor'))
- grad_w_query: float32 [768, 768], P('dp', 'tensor')
- grad_w_key: float32 [768, 768], P('dp', 'tensor')
- grad_w_value: float32 [768, 768], P('dp', 'tensor')
- grad_w_out: float32 [768, 768], P('tensor', 'dp')
- grad_w_up: float32 [768, 3072], P('dp', 'tensor')
- grad_w_down: float32 [3072, 768], P('tensor', 'dp')
- grad_b_query: float32 [12, 64], P('tensor', 'dp')
- grad_b_value: float32 [12, 64], P('tensor', 'dp')
- grad_b_up: float32 [24, 128], P('tensor', 'dp')
- grad_b_out: float32 [768], P(('dp', 'tensor'))
- grad_b_down: float32 [768], P(('dp', 'tensor'))
- grad_gain_one: float32 [768], P(('dp', 'tensor'))
- grad_shift_one: float32 [768], P(('dp', 'tensor'))
- grad_gain_two: float32 [768], P(('dp', 'tensor'))
- grad_shift_two: float32 [768], P(('dp', 'tensor'))
Inputs may be any that keep to these rules, and one draw needn't show every extreme that they name: `doc_lengths`: each row holds the 16 document lengths of one sequence in order and sums to 1024.
All inputs are finite; a program needn't handle non-finite values.
Results may differ from a plain program's by a relative error of at most 0.02.
Values may be sent and summed in bfloat16 or wider, within the bound.
No kernel may reach another device: no remote copies, remote signals or barrier semaphores. Data moves between devices by JAX's collectives and lax.ppermute only.
A program may use at most 192 MiB of HBM per device.

v0:
```python
import jax
import jax.numpy as jnp
from jax import lax
from jax.sharding import PartitionSpec as P

HD = 64
LEN = 1024
epsilon = 1e-06
root_half = 0.7071067811865476
inv_root_tau = 0.3989422804014327
masked_value = -1e30


def normalize(values, norm_gain, norm_shift):
    average = jnp.mean(values, axis=-1, keepdims=True)
    centred = values - average
    variance = jnp.mean(centred * centred, axis=-1, keepdims=True)
    inv_scale = lax.rsqrt(variance + epsilon)
    unit_rows = centred * inv_scale
    return (unit_rows * norm_gain + norm_shift, unit_rows, inv_scale)


def normalize_back(grad_out, unit_rows, inv_scale, norm_gain):
    grad_unit = grad_out * norm_gain
    middle = grad_unit - jnp.mean(grad_unit, axis=-1, keepdims=True)
    middle = middle - unit_rows * jnp.mean(grad_unit * unit_rows, axis=-1, keepdims=True)
    return inv_scale * middle


def gelu_parts(up_pre):
    normal_cdf = 0.5 * (1.0 + lax.erf(up_pre * root_half))
    return (
        up_pre * normal_cdf,
        normal_cdf + up_pre * inv_root_tau * jnp.exp(-0.5 * up_pre * up_pre),
    )


def segment_ids(doc_lengths, length):
    bounds = jnp.cumsum(doc_lengths, axis=-1)
    places = lax.broadcasted_iota(jnp.int32, (1, length, 1), 1)
    return jnp.sum((bounds[:, None, :] <= places).astype(jnp.int32), axis=-1)


def block_scores(query_block, key_seq, seg_block, seg_seq):
    scale = query_block.shape[-1] ** (-0.5)
    scores = (
        jnp.einsum("qhd,khd->hqk", query_block, key_seq, preferred_element_type=jnp.float32) * scale
    )
    allowed = seg_block[:, None] == seg_seq[None, :]
    return jnp.where(allowed[None], scores, masked_value)


def attention_forward(queries, keys_all, values_all, segments):
    seq_count, length = segments.shape
    head_count = queries.shape[1] // HD
    block_rows = min(512, length)
    shaped = (seq_count, length, head_count, HD)

    def one_sequence(inputs):
        query_one, key_one, value_one, seg_one = inputs
        outputs = []
        totals = []
        for offset in range(0, length, block_rows):
            ending = offset + block_rows
            scores = block_scores(
                query_one[offset:ending], key_one, seg_one[offset:ending], seg_one
            )
            row_top = jnp.max(scores, axis=-1, keepdims=True)
            weights = jnp.exp(scores - row_top)
            row_total = jnp.sum(weights, axis=-1, keepdims=True)
            probability = (weights / row_total).astype(jnp.bfloat16)
            mixture = jnp.einsum(
                "hqk,khd->qhd", probability, value_one, preferred_element_type=jnp.float32
            )
            outputs.append(mixture.astype(jnp.bfloat16))
            totals.append(row_top[..., 0] + jnp.log(row_total[..., 0]))
        return (jnp.concatenate(outputs, axis=0), jnp.concatenate(totals, axis=1))

    mixture, log_totals = lax.map(
        one_sequence,
        (queries.reshape(shaped), keys_all.reshape(shaped), values_all.reshape(shaped), segments),
    )
    return (mixture.reshape(seq_count * length, head_count * HD), log_totals)


def attention_backward(queries, keys_all, values_all, segments, log_totals, grad_mixture):
    seq_count, length = segments.shape
    head_count = queries.shape[1] // HD
    block_rows = min(512, length)
    shaped = (seq_count, length, head_count, HD)
    scale = HD ** (-0.5)

    def one_sequence(inputs):
        query_one, key_one, value_one, seg_one, grad_one, total_one = inputs
        grad_keys = jnp.zeros(key_one.shape, jnp.float32)
        grad_values = jnp.zeros(value_one.shape, jnp.float32)
        grad_queries = []
        for offset in range(0, length, block_rows):
            ending = offset + block_rows
            scores = block_scores(
                query_one[offset:ending], key_one, seg_one[offset:ending], seg_one
            )
            probability = jnp.exp(scores - total_one[:, offset:ending, None])
            grad_block = grad_one[offset:ending]
            grad_prob = jnp.einsum(
                "qhd,khd->hqk", grad_block, value_one, preferred_element_type=jnp.float32
            )
            inner = jnp.sum(probability * grad_prob, axis=-1, keepdims=True)
            grad_scores = (probability * (grad_prob - inner)).astype(jnp.bfloat16)
            block_query = jnp.einsum(
                "hqk,khd->qhd", grad_scores, key_one, preferred_element_type=jnp.float32
            )
            grad_queries.append((block_query * scale).astype(jnp.bfloat16))
            grad_keys = (
                grad_keys
                + jnp.einsum(
                    "hqk,qhd->khd",
                    grad_scores,
                    query_one[offset:ending],
                    preferred_element_type=jnp.float32,
                )
                * scale
            )
            grad_values = grad_values + jnp.einsum(
                "hqk,qhd->khd",
                probability.astype(jnp.bfloat16),
                grad_block,
                preferred_element_type=jnp.float32,
            )
        return (
            jnp.concatenate(grad_queries, axis=0),
            grad_keys.astype(jnp.bfloat16),
            grad_values.astype(jnp.bfloat16),
        )

    grad_q, grad_k, grad_v = lax.map(
        one_sequence,
        (
            queries.reshape(shaped),
            keys_all.reshape(shaped),
            values_all.reshape(shaped),
            segments,
            grad_mixture.reshape(shaped),
            log_totals,
        ),
    )
    flat = (seq_count * length, head_count * HD)
    return (grad_q.reshape(flat), grad_k.reshape(flat), grad_v.reshape(flat))


def per_device(
    tokens,
    doc_lengths,
    w_query,
    w_key,
    w_value,
    w_out,
    w_up,
    w_down,
    b_query,
    b_value,
    b_up,
    b_out,
    b_down,
    gain_one,
    shift_one,
    gain_two,
    shift_two,
    cotangent,
):
    segments = segment_ids(doc_lengths, LEN)
    gathered = (
        lax.all_gather(w_query, "dp", axis=0, tiled=True),
        lax.all_gather(w_key, "dp", axis=0, tiled=True),
        lax.all_gather(w_value, "dp", axis=0, tiled=True),
        lax.all_gather(w_out, "dp", axis=1, tiled=True),
        lax.all_gather(w_up, "dp", axis=0, tiled=True),
        lax.all_gather(w_down, "dp", axis=1, tiled=True),
        lax.all_gather(b_query, "dp", axis=1, tiled=True),
        lax.all_gather(b_value, "dp", axis=1, tiled=True),
        lax.all_gather(b_up, "dp", axis=1, tiled=True),
    )
    (
        full_query,
        full_key,
        full_value,
        full_out,
        full_up,
        full_down,
        bias_query,
        bias_value,
        bias_up,
    ) = gathered
    vectors = (
        lax.all_gather(b_out, ("dp", "tensor"), axis=0, tiled=True),
        lax.all_gather(b_down, ("dp", "tensor"), axis=0, tiled=True),
        lax.all_gather(gain_one, ("dp", "tensor"), axis=0, tiled=True),
        lax.all_gather(shift_one, ("dp", "tensor"), axis=0, tiled=True),
        lax.all_gather(gain_two, ("dp", "tensor"), axis=0, tiled=True),
        lax.all_gather(shift_two, ("dp", "tensor"), axis=0, tiled=True),
    )
    bias_out, bias_down, norm_gain_one, norm_shift_one, norm_gain_two, norm_shift_two = vectors
    local_rows = tokens.shape[0]
    tokens_all = lax.all_gather(tokens, "tensor", axis=0, tiled=True)
    queries = (
        jnp.dot(tokens_all, full_query, preferred_element_type=jnp.float32)
        + bias_query.reshape(-1).astype(jnp.float32)
    ).astype(jnp.bfloat16)
    keys_all = jnp.dot(tokens_all, full_key, preferred_element_type=jnp.float32).astype(
        jnp.bfloat16
    )
    values_all = (
        jnp.dot(tokens_all, full_value, preferred_element_type=jnp.float32)
        + bias_value.reshape(-1).astype(jnp.float32)
    ).astype(jnp.bfloat16)
    mixture, log_totals = attention_forward(queries, keys_all, values_all, segments)
    piece = lax.slice_in_dim(mixture, 0, local_rows * lax.axis_size("tensor"), axis=0)
    attn_part = lax.psum_scatter(
        jnp.dot(piece, full_out, preferred_element_type=jnp.float32).astype(jnp.bfloat16),
        "tensor",
        scatter_dimension=0,
        tiled=True,
    ).astype(jnp.float32)
    residual_one = attn_part + bias_out + tokens.astype(jnp.float32)
    first, unit_one, scale_one = normalize(residual_one, norm_gain_one, norm_shift_one)
    first_all = lax.all_gather(first.astype(jnp.bfloat16), "tensor", axis=0, tiled=True)
    up_pre = jnp.dot(first_all, full_up, preferred_element_type=jnp.float32) + bias_up.reshape(
        -1
    ).astype(jnp.float32)
    activated, slope = gelu_parts(up_pre)
    activated = activated.astype(jnp.bfloat16)
    piece = lax.slice_in_dim(activated, 0, local_rows * lax.axis_size("tensor"), axis=0)
    ffn_part = lax.psum_scatter(
        jnp.dot(piece, full_down, preferred_element_type=jnp.float32).astype(jnp.bfloat16),
        "tensor",
        scatter_dimension=0,
        tiled=True,
    ).astype(jnp.float32)
    residual_two = ffn_part + bias_down + first
    result, unit_two, scale_two = normalize(residual_two, norm_gain_two, norm_shift_two)
    grad_out = cotangent.astype(jnp.float32)
    grad_two = normalize_back(grad_out, unit_two, scale_two, norm_gain_two)
    grad_gain_two = jnp.sum(grad_out * unit_two, axis=0)
    grad_shift_two = jnp.sum(grad_out, axis=0)
    grad_bias_down = jnp.sum(grad_two, axis=0)
    grad_two_all = lax.all_gather(grad_two.astype(jnp.bfloat16), "tensor", axis=0, tiled=True)
    grad_w_down = jnp.einsum(
        "tf,td->fd", activated, grad_two_all, preferred_element_type=jnp.float32
    )
    grad_active = jnp.einsum(
        "td,fd->tf", grad_two_all, full_down, preferred_element_type=jnp.float32
    )
    grad_up = (grad_active * slope).astype(jnp.bfloat16)
    grad_bias_up = jnp.sum(grad_up, axis=0, dtype=jnp.float32)
    grad_w_up = jnp.einsum("td,tf->df", first_all, grad_up, preferred_element_type=jnp.float32)
    piece = lax.slice_in_dim(grad_up, 0, local_rows * lax.axis_size("tensor"), axis=0)
    grad_first = (
        lax.psum_scatter(
            jnp.einsum("tf,df->td", piece, full_up, preferred_element_type=jnp.float32).astype(
                jnp.bfloat16
            ),
            "tensor",
            scatter_dimension=0,
            tiled=True,
        ).astype(jnp.float32)
        + grad_two
    )
    grad_one = normalize_back(grad_first, unit_one, scale_one, norm_gain_one)
    grad_gain_one = jnp.sum(grad_first * unit_one, axis=0)
    grad_shift_one = jnp.sum(grad_first, axis=0)
    grad_bias_out = jnp.sum(grad_one, axis=0)
    grad_one_all = lax.all_gather(grad_one.astype(jnp.bfloat16), "tensor", axis=0, tiled=True)
    grad_w_out = jnp.einsum("th,td->hd", mixture, grad_one_all, preferred_element_type=jnp.float32)
    grad_mixture = jnp.einsum(
        "td,hd->th", grad_one_all, full_out, preferred_element_type=jnp.float32
    ).astype(jnp.bfloat16)
    grad_queries, grad_keys, grad_values = attention_backward(
        queries, keys_all, values_all, segments, log_totals, grad_mixture
    )
    grad_bias_query = jnp.sum(grad_queries, axis=0, dtype=jnp.float32)
    grad_bias_value = jnp.sum(grad_values, axis=0, dtype=jnp.float32)
    grad_w_query = jnp.einsum(
        "td,th->dh", tokens_all, grad_queries, preferred_element_type=jnp.float32
    )
    grad_w_key = jnp.einsum("td,th->dh", tokens_all, grad_keys, preferred_element_type=jnp.float32)
    grad_w_value = jnp.einsum(
        "td,th->dh", tokens_all, grad_values, preferred_element_type=jnp.float32
    )
    part_query = lax.slice_in_dim(grad_queries, 0, local_rows * lax.axis_size("tensor"), axis=0)
    part_key = lax.slice_in_dim(grad_keys, 0, local_rows * lax.axis_size("tensor"), axis=0)
    part_value = lax.slice_in_dim(grad_values, 0, local_rows * lax.axis_size("tensor"), axis=0)
    summed = jnp.einsum("th,dh->td", part_query, full_query, preferred_element_type=jnp.float32)
    summed = summed + jnp.einsum(
        "th,dh->td", part_key, full_key, preferred_element_type=jnp.float32
    )
    grad_input = (
        lax.psum_scatter(
            (
                summed
                + jnp.einsum(
                    "th,dh->td", part_value, full_value, preferred_element_type=jnp.float32
                )
            ).astype(jnp.bfloat16),
            "tensor",
            scatter_dimension=0,
            tiled=True,
        ).astype(jnp.float32)
        + grad_one
    )
    sent = (
        lax.psum_scatter(grad_w_query, "dp", scatter_dimension=0, tiled=True),
        lax.psum_scatter(grad_w_key, "dp", scatter_dimension=0, tiled=True),
        lax.psum_scatter(grad_w_value, "dp", scatter_dimension=0, tiled=True),
        lax.psum_scatter(grad_w_out, "dp", scatter_dimension=1, tiled=True),
        lax.psum_scatter(grad_w_up, "dp", scatter_dimension=0, tiled=True),
        lax.psum_scatter(grad_w_down, "dp", scatter_dimension=1, tiled=True),
        lax.psum_scatter(grad_bias_query.reshape(-1, HD), "dp", scatter_dimension=1, tiled=True),
        lax.psum_scatter(grad_bias_value.reshape(-1, HD), "dp", scatter_dimension=1, tiled=True),
        lax.psum_scatter(grad_bias_up.reshape(-1, 128), "dp", scatter_dimension=1, tiled=True),
    )
    vector_sums = (
        lax.psum_scatter(grad_bias_out, ("dp", "tensor"), scatter_dimension=0, tiled=True),
        lax.psum_scatter(grad_bias_down, ("dp", "tensor"), scatter_dimension=0, tiled=True),
        lax.psum_scatter(grad_gain_one, ("dp", "tensor"), scatter_dimension=0, tiled=True),
        lax.psum_scatter(grad_shift_one, ("dp", "tensor"), scatter_dimension=0, tiled=True),
        lax.psum_scatter(grad_gain_two, ("dp", "tensor"), scatter_dimension=0, tiled=True),
        lax.psum_scatter(grad_shift_two, ("dp", "tensor"), scatter_dimension=0, tiled=True),
    )
    return (
        result.astype(jnp.bfloat16),
        grad_input.astype(jnp.bfloat16),
        sent[0],
        sent[1],
        sent[2],
        sent[3],
        sent[4],
        sent[5],
        sent[6],
        sent[7],
        sent[8],
        vector_sums[0],
        vector_sums[1],
        vector_sums[2],
        vector_sums[3],
        vector_sums[4],
        vector_sums[5],
    )


def solution(mesh):
    placed = (
        P(("dp", "tensor"), None),
        P("dp", None),
        P("dp", "tensor"),
        P("dp", "tensor"),
        P("dp", "tensor"),
        P("tensor", "dp"),
        P("dp", "tensor"),
        P("tensor", "dp"),
        P("tensor", "dp"),
        P("tensor", "dp"),
        P("tensor", "dp"),
        P(("dp", "tensor")),
        P(("dp", "tensor")),
        P(("dp", "tensor")),
        P(("dp", "tensor")),
        P(("dp", "tensor")),
        P(("dp", "tensor")),
        P(("dp", "tensor"), None),
    )
    return jax.shard_map(
        per_device,
        mesh=mesh,
        in_specs=placed,
        out_specs=(
            P(("dp", "tensor"), None),
            P(("dp", "tensor"), None),
            P("dp", "tensor"),
            P("dp", "tensor"),
            P("dp", "tensor"),
            P("tensor", "dp"),
            P("dp", "tensor"),
            P("tensor", "dp"),
            P("tensor", "dp"),
            P("tensor", "dp"),
            P("tensor", "dp"),
            P(("dp", "tensor")),
            P(("dp", "tensor")),
            P(("dp", "tensor")),
            P(("dp", "tensor")),
            P(("dp", "tensor")),
            P(("dp", "tensor")),
        ),
        check_vma=False,
    )
```

profile of v0, /device:TPU:0, one launch (start us, length us, event | category | flops | bytes accessed | tf_op | source)
XLA Modules:
  0.0 1349.3 jit_solution(8543374420555080612)
XLA Ops:
  9.7 22.5 %all-gather.1 = bf16[8,8,3]{1,2,0:T(4,128)(2,1)S(1)} all-gather(bf16[1,8,3]{1,2,0:T(4,128)(2,1)} %bitcast.319), channel_id=1, replica_groups=mesh['dp'=8,'tensor'=4] {'dp'}, dimensions={0}, use_global_device_ids=true | all-gather | bytes 432 | tf_op jit(solution)/shard_map/all_gather | solution.py:179
  32.9 16.6 %all-gather = bf16[8,8,3]{1,2,0:T(4,128)(2,1)S(1)} all-gather(bf16[1,8,3]{1,2,0:T(4,128)(2,1)} %bitcast.320), channel_id=1, replica_groups=mesh['dp'=8,'tensor'=4] {'dp'}, dimensions={0}, use_global_device_ids=true | all-gather | bytes 432 | tf_op jit(solution)/shard_map/all_gather | solution.py:180
  50.7 31.2 %all_gather.63 = bf16[192,768]{0,1:T(8,128)(2,1)S(1)} all-gather(bf16[192,96]{0,1:T(8,128)(2,1)S(1)} %copy.104), channel_id=1, replica_groups=mesh['dp'=8,'tensor'=4] {'dp'}, dimensions={1}, use_global_device_ids=true | all-gather | bytes 331776 | tf_op jit(solution)/shard_map/all_gather | solution.py:176
  81.9 33.3 %all_gather.60 = bf16[768,192]{1,0:T(8,128)(2,1)} all-gather(bf16[96,192]{1,0:T(8,128)(2,1)} %param.24), channel_id=1, replica_groups=mesh['dp'=8,'tensor'=4] {'dp'}, dimensions={0}, use_global_device_ids=true | all-gather | bytes 331776 | tf_op jit(solution)/shard_map/all_gather | solution.py:173
  115.2 33.3 %all_gather.62 = bf16[768,192]{1,0:T(8,128)(2,1)} all-gather(bf16[96,192]{1,0:T(8,128)(2,1)} %param.25), channel_id=1, replica_groups=mesh['dp'=8,'tensor'=4] {'dp'}, dimensions={0}, use_global_device_ids=true | all-gather | bytes 331776 | tf_op jit(solution)/shard_map/all_gather | solution.py:174
  148.6 31.0 %all_gather.58 = bf16[768,192]{1,0:T(8,128)(2,1)S(1)} all-gather(bf16[96,192]{1,0:T(8,128)(2,1)S(1)} %copy-done.38), channel_id=1, replica_groups=mesh['dp'=8,'tensor'=4] {'dp'}, dimensions={0}, use_global_device_ids=true | all-gather | bytes 331776 | tf_op jit(solution)/shard_map/all_gather | solution.py:175
  205.9 52.6 %while.26 = (s32[]{:T(128)}, bf16[4,1024,3,64]{1,3,2,0:T(8,128)(2,1)}, f32[4,3,1024]{2,1,0:T(4,128)}, bf16[4,1024,3,64]{1,3,2,0:T(8,128)(2,1)}, s32[4,1024]{1,0:...) while((s32[]{:T(128)}, ...), condition=%wide.region_7.8_spmd, body=%wide.region_2.7_spmd.sunk | while | flops 845086720 | bytes 51542704 | solution.py:79
  278.5 39.3 %all-reduce.15 = (f32[768]{0:T(1024)}, f32[768]{0:T(1024)}, f32[768]{0:T(1024)}, f32[768]{0:T(1024)}, f32[768]{0:T(1024)}) all-reduce(f32[768]{0:T(1024)} %dynamic-update-slice.2, f32[768]{0:T(1024)} %dynamic-update-slice.1, f32[768]{0:T(1024)} %dynamic-update-slice, ...), channel_id=1, replica_groups=mesh['dp'=8,'tensor'=4] {'dp','tensor'}, use_global_device_ids=true, to_apply=%add.2 | all-reduce | flops 3840 | bytes 30720
  332.2 26.1 %all-gather.2 = bf16[8,16,6]{1,2,0:T(8,128)(2,1)S(1)} all-gather(bf16[1,16,6]{1,2,0:T(8,128)(2,1)} %bitcast.318), channel_id=1, replica_groups=mesh['dp'=8,'tensor'=4] {'dp'}, dimensions={0}, use_global_device_ids=true | all-gather | bytes 1728 | tf_op jit(solution)/shard_map/all_gather | solution.py:181
  360.4 17.5 %all-gather.12.cloned.1.call-done = bf16[4096,768]{1,0:T(8,128)(2,1)} async-done(((bf16[1024,768]{1,0:T(8,128)(2,1)}), bf16[4096,768]{1,0:T(8,128)(2,1)}) %all-gather.12.cloned.1.call-update) | async-done | bytes 6291472 | tf_op jit(solution)/shard_map/all_gather | solution.py:226
  390.0 31.7 %all-gather.16.cloned.1.call-done = bf16[768,768]{0,1:T(8,128)(2,1)} async-done(((bf16[768,96]{0,1:T(8,128)(2,1)}), bf16[768,768]{0,1:T(8,128)(2,1)}) %all-gather.16.cloned.1.call-update) | async-done | bytes 1179664 | tf_op jit(solution)/shard_map/all_gather | solution.py:178
  431.0 56.8 %reduce-scatter.26.cloned.1.call-done = bf16[1024,768]{1,0:T(8,128)(2,1)} async-done(((bf16[4096,768]{1,0:T(8,128)(2,1)}), bf16[1024,768]{1,0:T(8,128)(2,1)}) %reduce-scatter.26.cloned.1.call-update) | async-done | bytes 1572880 | tf_op jit(solution)/shard_map/reduce_scatter | solution.py:233
  498.6 46.5 %all-gather.18.cloned.1.call-done = bf16[4096,768]{1,0:T(8,128)(2,1)} async-done(((bf16[1024,768]{1,0:T(8,128)(2,1)}), bf16[4096,768]{1,0:T(8,128)(2,1)}) %all-gather.18.cloned.1.call-update) | async-done | bytes 6291472 | tf_op jit(solution)/shard_map/all_gather | solution.py:246
  567.9 58.3 %reduce-scatter.28.cloned.1.call-done = bf16[1024,768]{1,0:T(8,128)(2,1)} async-done(((bf16[4096,768]{1,0:T(8,128)(2,1)}), bf16[1024,768]{1,0:T(8,128)(2,1)}) %reduce-scatter.28.cloned.1.call-update) | async-done | bytes 1572880 | tf_op jit(solution)/shard_map/reduce_scatter | solution.py:258
  636.2 45.0 %all-gather.20.cloned.1.call-done = bf16[4096,768]{1,0:T(8,128)(2,1)} async-done(((bf16[1024,768]{1,0:T(8,128)(2,1)}), bf16[4096,768]{1,0:T(8,128)(2,1)}) %all-gather.20.cloned.1.call-update) | async-done | bytes 6291472 | tf_op jit(solution)/shard_map/all_gather | solution.py:272
  694.5 154.3 %while.27 = (s32[]{:T(128)}, bf16[4,1024,3,64]{1,3,2,0:T(8,128)(2,1)}, bf16[4,1024,3,64]{1,3,2,0:T(8,128)(2,1)}, bf16[4,1024,3,64]{1,3,2,0:T(8,128)(2,1)S(1)}, b...) while((s32[]{:T(128)}, ...), condition=%wide.region_22.23_spmd, body=%wide.region_19.22_spmd.sunk | while | flops 2063660032 | bytes 151801680 | solution.py:136
  936.8 21.6 %all-reduce.16 = (f32[3,64]{1,0:T(4,128)S(1)}, f32[3,64]{1,0:T(4,128)S(1)}) all-reduce(f32[3,64]{1,0:T(4,128)S(1)} %convert_reduce_fusion.3, f32[3,64]{1,0:T(4,128)S(1)} %convert_reduce_fusion.2), channel_id=12, replica_groups=mesh['dp'=8,'tensor'=4] {'dp'}, use_global_device_ids=true, to_apply=%region_31.32.clone | all-reduce | flops 384 | bytes 3072
  961.3 37.0 %reduce-scatter.30.cloned.1.call-done = bf16[1024,768]{1,0:T(8,128)(2,1)} async-done(((bf16[4096,768]{1,0:T(8,128)(2,1)}), bf16[1024,768]{1,0:T(8,128)(2,1)}) %reduce-scatter.30.cloned.1.call-update) | async-done | bytes 1572880 | tf_op jit(solution)/shard_map/reduce_scatter | solution.py:297
  1002.5 40.5 %all-reduce.14 = (f32[768]{0:T(1024)S(1)}, f32[768]{0:T(1024)S(1)}, f32[768]{0:T(1024)S(1)}, f32[768]{0:T(1024)S(1)}, f32[768]{0:T(1024)S(1)}, /*index=5*/f32[768]{0:T(1024)S(1)}, f32[768]{0:T(1024)S(1)}) all-reduce(f32[768]{0:T(1024)S(1)} %dynamic-update-slice.5, ...), channel_id=1, replica_groups=mesh['dp'=8,'tensor'=4] {'dp','tensor'}, use_global_device_ids=true, to_apply=%add.5 | all-reduce | flops 5376 | bytes 43008
  1048.2 24.0 %reduce-scatter.32.cloned.1.call-done = f32[96,768]{1,0:T(8,128)} async-done(((f32[768,768]{1,0:T(8,128)}), f32[96,768]{1,0:T(8,128)}) %reduce-scatter.32.cloned.1.call-update) | async-done | bytes 294928 | tf_op jit(solution)/shard_map/reduce_scatter | solution.py:315
  1072.2 72.5 %reduce-scatter.34.cloned.1.call-done = f32[768,96]{0,1:T(8,128)} async-done(((f32[768,768]{0,1:T(8,128)}), f32[768,96]{0,1:T(8,128)}) %reduce-scatter.34.cloned.1.call-update) | async-done | bytes 294928 | tf_op jit(solution)/shard_map/reduce_scatter | solution.py:316
  1144.7 65.8 %reduce-scatter.36.cloned.1.call-done = f32[96,192]{1,0:T(8,128)} async-done(((f32[768,192]{1,0:T(8,128)}), f32[96,192]{1,0:T(8,128)}) %reduce-scatter.36.cloned.1.call-update) | async-done | bytes 73744
  1210.5 65.5 %reduce-scatter.38.cloned.1.call-done = f32[96,192]{1,0:T(8,128)} async-done(((f32[768,192]{1,0:T(8,128)}), f32[96,192]{1,0:T(8,128)}) %reduce-scatter.38.cloned.1.call-update) | async-done | bytes 73744
  1276.0 65.7 %reduce-scatter.40.cloned.1.call-done = f32[96,192]{1,0:T(8,128)} async-done(((f32[768,192]{1,0:T(8,128)}), f32[96,192]{1,0:T(8,128)}) %reduce-scatter.40.cloned.1.call-update) | async-done | bytes 73744
  (403 shorter events, 448.9 us)
Async XLA Ops:
  8.0 140.5 %copy-start.38 = (bf16[96,192]{1,0:T(8,128)(2,1)S(1)}, bf16[96,192]{1,0:T(8,128)(2,1)}, u32[]{:S(2)}) copy-start(bf16[96,192]{1,0:T(8,128)(2,1)} %param.26) | copy-start | bytes 110596
  8.0 171.5 %all-gather.10.cloned.1.call-start = ((), (), s32[]{:S(2)}) async-start(), calls=%async_computation.11 | async-start | bytes 7864320 | tf_op jit(solution)/shard_map/all_gather | solution.py:204
  8.8 317.1 %reduce-scatter.24.cloned.1.call-start = ((), (), s32[]{:S(2)}) async-start(), calls=%async_computation.12 | async-start | bytes 7864320 | tf_op jit(solution)/shard_map/reduce_scatter | solution.py:218
  268.0 57.9 %copy-start.5 = (bf16[1024,768]{1,0:T(8,128)(2,1)S(1)}, bf16[1024,768]{1,0:T(8,128)(2,1)}, u32[]{:S(2)}) copy-start(bf16[1024,768]{1,0:T(8,128)(2,1)} %param.22) | copy-start | bytes 4718596
  268.0 92.4 %all-gather.14.cloned.1.call-start = ((), (), s32[]{:S(2)}) async-start(), calls=%async_computation.14 | async-start | bytes 1327104 | tf_op jit(solution)/shard_map/all_gather | solution.py:177
  268.6 109.3 %all-gather.12.cloned.1.call-start = ((), (), s32[]{:S(2)}) async-start(), calls=%async_computation.13 | async-start | bytes 7864320 | tf_op jit(solution)/shard_map/all_gather | solution.py:226
  331.6 90.1 %all-gather.16.cloned.1.call-start = ((), (), s32[]{:S(2)}) async-start(), calls=%async_computation.15 | async-start | bytes 1327104 | tf_op jit(solution)/shard_map/all_gather | solution.py:178
  332.2 155.6 %reduce-scatter.26.cloned.1.call-start = ((), (), s32[]{:S(2)}) async-start(), calls=%async_computation.16 | async-start | bytes 7864320 | tf_op jit(solution)/shard_map/reduce_scatter | solution.py:233
  430.9 114.1 %all-gather.18.cloned.1.call-start = ((), (), s32[]{:S(2)}) async-start(), calls=%async_computation.17 | async-start | bytes 7864320 | tf_op jit(solution)/shard_map/all_gather | solution.py:246
  498.5 127.6 %reduce-scatter.28.cloned.1.call-start = ((), (), s32[]{:S(2)}) async-start(), calls=%async_computation.18 | async-start | bytes 7864320 | tf_op jit(solution)/shard_map/reduce_scatter | solution.py:258
  545.1 15.6 %copy-start.48 = (bf16[768,768]{1,0:T(8,128)(2,1)S(1)}, bf16[768,768]{1,0:T(8,128)(2,1)}, u32[]{:S(2)}) copy-start(bf16[768,768]{1,0:T(8,128)(2,1)} %all-gather.14.cloned.1.call-done) | copy-start | bytes 3538948
  567.8 113.4 %all-gather.20.cloned.1.call-start = ((), (), s32[]{:S(2)}) async-start(), calls=%async_computation.19 | async-start | bytes 7864320 | tf_op jit(solution)/shard_map/all_gather | solution.py:272
  634.6 292.5 %reduce-scatter.44.cloned.1.call-start = ((), (), s32[]{:S(2)}) async-start(), calls=%async_computation.27 | async-start | bytes 73728
  636.1 323.6 %reduce-scatter.42.cloned.1.call-start = ((), (), s32[]{:S(2)}) async-start(), calls=%async_computation.26 | async-start | bytes 884736
  876.0 122.4 %reduce-scatter.30.cloned.1.call-start = ((), (), s32[]{:S(2)}) async-start(), calls=%async_computation.20 | async-start | bytes 7864320 | tf_op jit(solution)/shard_map/reduce_scatter | solution.py:297
  889.5 182.7 %reduce-scatter.32.cloned.1.call-start = ((), (), s32[]{:S(2)}) async-start(), calls=%async_computation.21 | async-start | bytes 2654208 | tf_op jit(solution)/shard_map/reduce_scatter | solution.py:315
  899.7 245.0 %reduce-scatter.34.cloned.1.call-start = ((), (), s32[]{:S(2)}) async-start(), calls=%async_computation.22 | async-start | bytes 2654208 | tf_op jit(solution)/shard_map/reduce_scatter | solution.py:316
  909.9 300.6 %reduce-scatter.36.cloned.1.call-start = ((), (), s32[]{:S(2)}) async-start(), calls=%async_computation.23 | async-start | bytes 884736
  917.7 358.3 %reduce-scatter.38.cloned.1.call-start = ((), (), s32[]{:S(2)}) async-start(), calls=%async_computation.24 | async-start | bytes 884736
  925.6 416.2 %reduce-scatter.40.cloned.1.call-start = ((), (), s32[]{:S(2)}) async-start(), calls=%async_computation.25 | async-start | bytes 884736
  998.4 48.1 %copy-start.4 = (f32[1024,768]{1,0:T(8,128)S(1)}, f32[1024,768]{1,0:T(8,128)}, u32[]{:S(2)}) copy-start(f32[1024,768]{1,0:T(8,128)} %copy-done.3) | copy-start | bytes 9437188
  998.4 48.1 %copy-start.33 = (f32[1024]{0:T(1024)S(1)}, f32[1024]{0:T(1024)}, u32[]{:S(2)}) copy-start(f32[1024]{0:T(1024)} %copy-done.32) | copy-start | bytes 12292
  998.4 48.1 %copy-start.37 = (f32[1024]{0:T(1024)S(1)}, f32[1024]{0:T(1024)}, u32[]{:S(2)}) copy-start(f32[1024]{0:T(1024)} %copy-done.36) | copy-start | bytes 12292
  998.4 48.1 %copy-start.40 = (f32[768]{0:T(1024)S(1)}, f32[768]{0:T(1024)}, u32[]{:S(2)}) copy-start(f32[768]{0:T(1024)} %get-tuple-element.338) | copy-start | bytes 9220
  (68 other events, 269.5 us)
Sparse Core Ops, SparseCore 0:
  10.4 49.0 all-gather.9
  268.1 57.7 reduce-scatter.23
  498.6 46.3 all-gather.17
  634.8 46.3 all-gather.19
Sparse Core Ops, SparseCore 1:
  270.9 39.8 all-gather.13
  331.7 46.1 all-gather.11
  380.2 41.5 all-gather.15
  431.0 56.7 reduce-scatter.25
  567.9 58.2 reduce-scatter.27
  639.8 61.4 reduce-scatter.43
  876.1 62.5 reduce-scatter.41
  941.1 57.2 reduce-scatter.29
  1002.7 69.4 reduce-scatter.31
  1076.7 68.0 reduce-scatter.33
  1148.8 61.6 reduce-scatter.35
  1214.4 61.6 reduce-scatter.37
  1280.1 61.5 reduce-scatter.39
where the time goes:
time: 1360 us; the launch traced here: 1350 us
  waiting for transfers between devices  596 us (44%)
  blocking collectives  295 us (22%)
  matrix products  276 us (20%)
  other arithmetic  88.6 us (7%)
  local copies, waits for them, and re-layouts  73.7 us (5%)
  between operations  17.1 us (1%)
    unnamed x22, waiting for transfers between devices  199 us
    unnamed x3, blocking collectives  101 us
    reduce_scatter x1, waiting for transfers between devices, per_device(): lax.psum_scatter(grad_w_down, 'dp', scatter_dimension=1, tiled=True)  72.5 us
    reduce_scatter x1, waiting for transfers between devices, per_device(): lax.psum_scatter(jnp.einsum('tf,df->td', piece, full_up, preferred_elemen...  58.3 us
    reduce_scatter x1, waiting for transfers between devices, per_device(): lax.psum_scatter(jnp.dot(piece, full_down, preferred_element_type=jnp.flo...  56.8 us
    all_gather x1, waiting for transfers between devices, per_device(): lax.all_gather(grad_two.astype(jnp.bfloat16), 'tensor', axis=0, tiled=True)  46.5 us
    all_gather x1, waiting for transfers between devices, per_device(): lax.all_gather(grad_one.astype(jnp.bfloat16), 'tensor', axis=0, tiled=True)  45 us
    dot_general x8, matrix products, one_sequence(): jnp.einsum('qhd,khd->hqk', grad_block, value_one, preferred_element_type=...  43.9 us
  transfers between devices with their start and end apart: 17, of which 13 were waited for; matrix products, arithmetic and copies ran while one was open for 22% of the time, Pallas kernels for 0%

commit v1 on v0

--- a/solution.py
+++ b/solution.py
@@ -9,6 +9,12 @@
 root_half = 0.7071067811865476
 inv_root_tau = 0.3989422804014327
 masked_value = -1e30
+
+
+def laid_out(blocks, dim):
+    blocks = jnp.moveaxis(blocks, 0, dim)
+    lengths = blocks.shape
+    return blocks.reshape(*lengths[:dim], lengths[dim] * lengths[dim + 1], *lengths[dim + 2 :])
 
 
 def normalize(values, norm_gain, norm_shift):
@@ -243,7 +249,20 @@
     grad_gain_two = jnp.sum(grad_out * unit_two, axis=0)
     grad_shift_two = jnp.sum(grad_out, axis=0)
     grad_bias_down = jnp.sum(grad_two, axis=0)
-    grad_two_all = lax.all_gather(grad_two.astype(jnp.bfloat16), "tensor", axis=0, tiled=True)
+    shard = grad_two.astype(jnp.bfloat16)
+    peers = lax.axis_size("tensor")
+    pairs = [(i, (i + 1) % peers) for i in range(peers)]
+    back = [(b, a) for a, b in pairs]
+    lower, upper = ([], [])
+    for step in range(peers - 1):
+        if step % 2 == 0:
+            lower.append(lax.ppermute(lower[-1] if lower else shard, "tensor", pairs))
+        else:
+            upper.append(lax.ppermute(upper[-1] if upper else shard, "tensor", back))
+    blocks = jnp.stack([*lower[::-1], shard, *upper])
+    shift = lax.axis_index("tensor") - len(lower)
+    blocks = blocks[(jnp.arange(peers) - shift) % peers]
+    grad_two_all = laid_out(blocks, 0)
     grad_w_down = jnp.einsum(
         "tf,td->fd", activated, grad_two_all, preferred_element_type=jnp.float32
     )

time: 1360 us -> 1380 us (1.015)
    ppermute x0 -> x3, waiting for transfers between devices: none -> 54.2 us  [the longest x2 54.2 us: per_device(): lower.append(lax.ppermute(lower[-1] if lower else shard, 'tensor', pairs))]
    all_gather x1 -> x0, waiting for transfers between devices: 46.5 us -> none  [per_device(): lax.all_gather(grad_two.astype(jnp.bfloat16), 'tensor', axis=0, tiled=True)]
    unnamed x22 -> x21, waiting for transfers between devices: 199 us -> 199 us
  transfers between devices with their start and end apart: 17 -> 19, of which waited for: 13 -> 14; matrix products, arithmetic and copies ran while one was open for 22% -> 22% of each run, Pallas kernels for 0% -> 0%
where the time goes in v1:
time: 1380 us; the launch traced here: 1370 us
  waiting for transfers between devices  604 us (44%)
  blocking collectives  295 us (21%)
  matrix products  275 us (20%)
  other arithmetic  96.1 us (7%)
  local copies, waits for them, and re-layouts  80 us (6%)
  between operations  17.1 us (1%)
    unnamed x21, waiting for transfers between devices  199 us
    unnamed x3, blocking collectives  101 us
    reduce_scatter x1, waiting for transfers between devices, per_device(): lax.psum_scatter(grad_w_down, 'dp', scatter_dimension=1, tiled=True)  72.6 us
    reduce_scatter x1, waiting for transfers between devices, per_device(): lax.psum_scatter(jnp.einsum('tf,df->td', piece, full_up, preferred_elemen...  58.2 us
    reduce_scatter x1, waiting for transfers between devices, per_device(): lax.psum_scatter(jnp.dot(piece, full_down, preferred_element_type=jnp.flo...  56.8 us
    ppermute x2, waiting for transfers between devices, per_device(): lower.append(lax.ppermute(lower[-1] if lower else shard, 'tensor', pairs))  54.2 us
    all_gather x1, waiting for transfers between devices, per_device(): lax.all_gather(grad_one.astype(jnp.bfloat16), 'tensor', axis=0, tiled=True)  44.8 us
    dot_general x8, matrix products, one_sequence(): jnp.einsum('qhd,khd->hqk', grad_block, value_one, preferred_element_type=...  44 us
  transfers between devices with their start and end apart: 19, of which 14 were waited for; matrix products, arithmetic and copies ran while one was open for 22% of the time, Pallas kernels for 0%

profile of v1, /device:TPU:0, one launch (start us, length us, event | category | flops | bytes accessed | tf_op | source)
XLA Modules:
  0.0 1372.2 jit_solution(13643082405039575554)
XLA Ops:
  9.7 22.5 %all-gather.1 = bf16[8,8,3]{1,2,0:T(4,128)(2,1)S(1)} all-gather(bf16[1,8,3]{1,2,0:T(4,128)(2,1)} %bitcast.328), channel_id=1, replica_groups=mesh['dp'=8,'tensor'=4] {'dp'}, dimensions={0}, use_global_device_ids=true | all-gather | bytes 432 | tf_op jit(solution)/shard_map/all_gather | solution.py:185
  50.7 31.2 %all_gather.60 = bf16[192,768]{0,1:T(8,128)(2,1)S(1)} all-gather(bf16[192,96]{0,1:T(8,128)(2,1)S(1)} %copy.104), channel_id=1, replica_groups=mesh['dp'=8,'tensor'=4] {'dp'}, dimensions={1}, use_global_device_ids=true | all-gather | bytes 331776 | tf_op jit(solution)/shard_map/all_gather | solution.py:182
  81.9 33.3 %all_gather.57 = bf16[768,192]{1,0:T(8,128)(2,1)} all-gather(bf16[96,192]{1,0:T(8,128)(2,1)} %param.24), channel_id=1, replica_groups=mesh['dp'=8,'tensor'=4] {'dp'}, dimensions={0}, use_global_device_ids=true | all-gather | bytes 331776 | tf_op jit(solution)/shard_map/all_gather | solution.py:179
  115.2 33.3 %all_gather.59 = bf16[768,192]{1,0:T(8,128)(2,1)} all-gather(bf16[96,192]{1,0:T(8,128)(2,1)} %param.25), channel_id=1, replica_groups=mesh['dp'=8,'tensor'=4] {'dp'}, dimensions={0}, use_global_device_ids=true | all-gather | bytes 331776 | tf_op jit(solution)/shard_map/all_gather | solution.py:180
  148.6 31.0 %all_gather.55 = bf16[768,192]{1,0:T(8,128)(2,1)S(1)} all-gather(bf16[96,192]{1,0:T(8,128)(2,1)S(1)} %copy-done.38), channel_id=1, replica_groups=mesh['dp'=8,'tensor'=4] {'dp'}, dimensions={0}, use_global_device_ids=true | all-gather | bytes 331776 | tf_op jit(solution)/shard_map/all_gather | solution.py:181
  205.9 52.6 %while.26 = (s32[]{:T(128)}, bf16[4,1024,3,64]{1,3,2,0:T(8,128)(2,1)}, f32[4,3,1024]{2,1,0:T(4,128)}, bf16[4,1024,3,64]{1,3,2,0:T(8,128)(2,1)}, s32[4,1024]{1,0:...) while((s32[]{:T(128)}, ...), condition=%wide.region_7.8_spmd, body=%wide.region_2.7_spmd.sunk | while | flops 845086720 | bytes 51542704 | solution.py:85
  278.4 39.3 %all-reduce.15 = (f32[768]{0:T(1024)}, f32[768]{0:T(1024)}, f32[768]{0:T(1024)}, f32[768]{0:T(1024)}, f32[768]{0:T(1024)}) all-reduce(f32[768]{0:T(1024)} %dynamic-update-slice.2, f32[768]{0:T(1024)} %dynamic-update-slice.1, f32[768]{0:T(1024)} %dynamic-update-slice, ...), channel_id=1, replica_groups=mesh['dp'=8,'tensor'=4] {'dp','tensor'}, use_global_device_ids=true, to_apply=%add.2 | all-reduce | flops 3840 | bytes 30720
  332.2 26.1 %all-gather.2 = bf16[8,16,6]{1,2,0:T(8,128)(2,1)S(1)} all-gather(bf16[1,16,6]{1,2,0:T(8,128)(2,1)} %bitcast.327), channel_id=1, replica_groups=mesh['dp'=8,'tensor'=4] {'dp'}, dimensions={0}, use_global_device_ids=true | all-gather | bytes 1728 | tf_op jit(solution)/shard_map/all_gather | solution.py:187
  360.4 17.5 %all-gather.11.cloned.1.call-done = bf16[4096,768]{1,0:T(8,128)(2,1)} async-done(((bf16[1024,768]{1,0:T(8,128)(2,1)}), bf16[4096,768]{1,0:T(8,128)(2,1)}) %all-gather.11.cloned.1.call-update) | async-done | bytes 6291472 | tf_op jit(solution)/shard_map/all_gather | solution.py:232
  389.9 31.7 %all-gather.15.cloned.1.call-done = bf16[768,768]{0,1:T(8,128)(2,1)} async-done(((bf16[768,96]{0,1:T(8,128)(2,1)}), bf16[768,768]{0,1:T(8,128)(2,1)}) %all-gather.15.cloned.1.call-update) | async-done | bytes 1179664 | tf_op jit(solution)/shard_map/all_gather | solution.py:184
  430.9 56.8 %reduce-scatter.26.cloned.1.call-done = bf16[1024,768]{1,0:T(8,128)(2,1)} async-done(((bf16[4096,768]{1,0:T(8,128)(2,1)}), bf16[1024,768]{1,0:T(8,128)(2,1)}) %reduce-scatter.26.cloned.1.call-update) | async-done | bytes 1572880 | tf_op jit(solution)/shard_map/reduce_scatter | solution.py:239
  500.2 34.7 %collective-permute-done = bf16[1024,768]{1,0:T(8,128)(2,1)} collective-permute-done((bf16[1024,768]{1,0:T(8,128)(2,1)}, bf16[1024,768]{1,0:T(8,128)(2,1)}, u32[]{:S(2)}, u32[]{:S(2)}) %collective-permute-start) | collective-permute-done | bytes 1572896 | tf_op jit(solution)/shard_map/ppermute | solution.py:259
  535.5 19.5 %collective-permute-done.1 = bf16[1024,768]{1,0:T(8,128)(2,1)} collective-permute-done((bf16[1024,768]{1,0:T(8,128)(2,1)}, bf16[1024,768]{1,0:T(8,128)(2,1)}, u32[]{:S(2)}, u32[]{:S(2)}) %collective-permute-start.1) | collective-permute-done | bytes 1572896 | tf_op jit(solution)/shard_map/ppermute | solution.py:259
  591.0 58.2 %reduce-scatter.28.cloned.1.call-done = bf16[1024,768]{1,0:T(8,128)(2,1)} async-done(((bf16[4096,768]{1,0:T(8,128)(2,1)}), bf16[1024,768]{1,0:T(8,128)(2,1)}) %reduce-scatter.28.cloned.1.call-update) | async-done | bytes 1572880 | tf_op jit(solution)/shard_map/reduce_scatter | solution.py:277
  659.3 44.8 %all-gather.17.cloned.1.call-done = bf16[4096,768]{1,0:T(8,128)(2,1)} async-done(((bf16[1024,768]{1,0:T(8,128)(2,1)}), bf16[4096,768]{1,0:T(8,128)(2,1)}) %all-gather.17.cloned.1.call-update) | async-done | bytes 6291472 | tf_op jit(solution)/shard_map/all_gather | solution.py:291
  717.3 154.3 %while.27 = (s32[]{:T(128)}, bf16[4,1024,3,64]{1,3,2,0:T(8,128)(2,1)}, bf16[4,1024,3,64]{1,3,2,0:T(8,128)(2,1)}, bf16[4,1024,3,64]{1,3,2,0:T(8,128)(2,1)S(1)}, b...) while((s32[]{:T(128)}, ...), condition=%wide.region_22.23_spmd, body=%wide.region_19.22_spmd.sunk | while | flops 2063660032 | bytes 151801680 | solution.py:142
  959.7 21.6 %all-reduce.16 = (f32[3,64]{1,0:T(4,128)S(1)}, f32[3,64]{1,0:T(4,128)S(1)}) all-reduce(f32[3,64]{1,0:T(4,128)S(1)} %convert_reduce_fusion.3, f32[3,64]{1,0:T(4,128)S(1)} %convert_reduce_fusion.2), channel_id=12, replica_groups=mesh['dp'=8,'tensor'=4] {'dp'}, use_global_device_ids=true, to_apply=%region_31.32.clone | all-reduce | flops 384 | bytes 3072
  984.2 37.0 %reduce-scatter.30.cloned.1.call-done = bf16[1024,768]{1,0:T(8,128)(2,1)} async-done(((bf16[4096,768]{1,0:T(8,128)(2,1)}), bf16[1024,768]{1,0:T(8,128)(2,1)}) %reduce-scatter.30.cloned.1.call-update) | async-done | bytes 1572880 | tf_op jit(solution)/shard_map/reduce_scatter | solution.py:316
  1025.4 40.5 %all-reduce.14 = (f32[768]{0:T(1024)S(1)}, f32[768]{0:T(1024)S(1)}, f32[768]{0:T(1024)S(1)}, f32[768]{0:T(1024)S(1)}, f32[768]{0:T(1024)S(1)}, /*index=5*/f32[768]{0:T(1024)S(1)}, f32[768]{0:T(1024)S(1)}) all-reduce(f32[768]{0:T(1024)S(1)} %dynamic-update-slice.5, ...), channel_id=1, replica_groups=mesh['dp'=8,'tensor'=4] {'dp','tensor'}, use_global_device_ids=true, to_apply=%add.5 | all-reduce | flops 5376 | bytes 43008
  1071.1 24.0 %reduce-scatter.32.cloned.1.call-done = f32[96,768]{1,0:T(8,128)} async-done(((f32[768,768]{1,0:T(8,128)}), f32[96,768]{1,0:T(8,128)}) %reduce-scatter.32.cloned.1.call-update) | async-done | bytes 294928 | tf_op jit(solution)/shard_map/reduce_scatter | solution.py:334
  1095.1 72.6 %reduce-scatter.34.cloned.1.call-done = f32[768,96]{0,1:T(8,128)} async-done(((f32[768,768]{0,1:T(8,128)}), f32[768,96]{0,1:T(8,128)}) %reduce-scatter.34.cloned.1.call-update) | async-done | bytes 294928 | tf_op jit(solution)/shard_map/reduce_scatter | solution.py:335
  1167.7 65.7 %reduce-scatter.36.cloned.1.call-done = f32[96,192]{1,0:T(8,128)} async-done(((f32[768,192]{1,0:T(8,128)}), f32[96,192]{1,0:T(8,128)}) %reduce-scatter.36.cloned.1.call-update) | async-done | bytes 73744
  1233.3 65.5 %reduce-scatter.38.cloned.1.call-done = f32[96,192]{1,0:T(8,128)} async-done(((f32[768,192]{1,0:T(8,128)}), f32[96,192]{1,0:T(8,128)}) %reduce-scatter.38.cloned.1.call-update) | async-done | bytes 73744
  1298.9 65.7 %reduce-scatter.40.cloned.1.call-done = f32[96,192]{1,0:T(8,128)} async-done(((f32[768,192]{1,0:T(8,128)}), f32[96,192]{1,0:T(8,128)}) %reduce-scatter.40.cloned.1.call-update) | async-done | bytes 73744
  (410 shorter events, 480.9 us)
Async XLA Ops:
  8.0 140.5 %copy-start.38 = (bf16[96,192]{1,0:T(8,128)(2,1)S(1)}, bf16[96,192]{1,0:T(8,128)(2,1)}, u32[]{:S(2)}) copy-start(bf16[96,192]{1,0:T(8,128)(2,1)} %param.26) | copy-start | bytes 110596
  8.0 171.5 %all-gather.9.cloned.1.call-start = ((), (), s32[]{:S(2)}) async-start(), calls=%async_computation.11 | async-start | bytes 7864320 | tf_op jit(solution)/shard_map/all_gather | solution.py:210
  8.8 317.1 %reduce-scatter.24.cloned.1.call-start = ((), (), s32[]{:S(2)}) async-start(), calls=%async_computation.12 | async-start | bytes 7864320 | tf_op jit(solution)/shard_map/reduce_scatter | solution.py:224
  267.9 57.9 %copy-start.5 = (bf16[1024,768]{1,0:T(8,128)(2,1)S(1)}, bf16[1024,768]{1,0:T(8,128)(2,1)}, u32[]{:S(2)}) copy-start(bf16[1024,768]{1,0:T(8,128)(2,1)} %param.22) | copy-start | bytes 4718596
  268.0 92.4 %all-gather.13.cloned.1.call-start = ((), (), s32[]{:S(2)}) async-start(), calls=%async_computation.14 | async-start | bytes 1327104 | tf_op jit(solution)/shard_map/all_gather | solution.py:183
  268.5 109.3 %all-gather.11.cloned.1.call-start = ((), (), s32[]{:S(2)}) async-start(), calls=%async_computation.13 | async-start | bytes 7864320 | tf_op jit(solution)/shard_map/all_gather | solution.py:232
  331.6 90.1 %all-gather.15.cloned.1.call-start = ((), (), s32[]{:S(2)}) async-start(), calls=%async_computation.15 | async-start | bytes 1327104 | tf_op jit(solution)/shard_map/all_gather | solution.py:184
  332.1 155.6 %reduce-scatter.26.cloned.1.call-start = ((), (), s32[]{:S(2)}) async-start(), calls=%async_computation.16 | async-start | bytes 7864320 | tf_op jit(solution)/shard_map/reduce_scatter | solution.py:239
  430.9 218.3 %reduce-scatter.28.cloned.1.call-start = ((), (), s32[]{:S(2)}) async-start(), calls=%async_computation.17 | async-start | bytes 7864320 | tf_op jit(solution)/shard_map/reduce_scatter | solution.py:277
  498.4 36.4 %collective-permute-start = (bf16[1024,768]{1,0:T(8,128)(2,1)}, bf16[1024,768]{1,0:T(8,128)(2,1)}, u32[]{:S(2)}, u32[]{:S(2)}) collective-permute-start(bf16[1024,768]{1,0:T(8,128)(2,1)} %get-tuple-element.343), channel_id=1, source_target_pairs={{0,1},{1,2},{2,3},{3,0},{4,5},{5,6},{6,7},{7,4},{8,9},{9,10},{10,1... | collective-permute-start | bytes 4718600 | tf_op jit(solution)/shard_map/ppermute | solution.py:259
  498.4 37.1 %collective-permute-start.2 = (bf16[1024,768]{1,0:T(8,128)(2,1)}, bf16[1024,768]{1,0:T(8,128)(2,1)}, u32[]{:S(2)}, u32[]{:S(2)}) collective-permute-start(bf16[1024,768]{1,0:T(8,128)(2,1)} %get-tuple-element.343), channel_id=1, source_target_pairs={{1,0},{2,1},{3,2},{0,3},{5,4},{6,5},{7,6},{4,7},{9,8},{10,9},{11,1... | collective-permute-start | bytes 4718600 | tf_op jit(solution)/shard_map/ppermute | solution.py:261
  534.9 20.2 %collective-permute-start.1 = (bf16[1024,768]{1,0:T(8,128)(2,1)}, bf16[1024,768]{1,0:T(8,128)(2,1)}, u32[]{:S(2)}, u32[]{:S(2)}) collective-permute-start(bf16[1024,768]{1,0:T(8,128)(2,1)} %collective-permute-done), channel_id=1, source_target_pairs={{0,1},{1,2},{2,3},{3,0},{4,5},{5,6},{6,7},{7,4},{8,9},{9,10},{10,1... | collective-permute-start | bytes 4718600 | tf_op jit(solution)/shard_map/ppermute | solution.py:259
  590.9 113.1 %all-gather.17.cloned.1.call-start = ((), (), s32[]{:S(2)}) async-start(), calls=%async_computation.18 | async-start | bytes 7864320 | tf_op jit(solution)/shard_map/all_gather | solution.py:291
  657.7 292.3 %reduce-scatter.44.cloned.1.call-start = ((), (), s32[]{:S(2)}) async-start(), calls=%async_computation.26 | async-start | bytes 73728
  659.2 323.4 %reduce-scatter.42.cloned.1.call-start = ((), (), s32[]{:S(2)}) async-start(), calls=%async_computation.25 | async-start | bytes 884736
  898.8 122.4 %reduce-scatter.30.cloned.1.call-start = ((), (), s32[]{:S(2)}) async-start(), calls=%async_computation.19 | async-start | bytes 7864320 | tf_op jit(solution)/shard_map/reduce_scatter | solution.py:316
  912.3 182.8 %reduce-scatter.32.cloned.1.call-start = ((), (), s32[]{:S(2)}) async-start(), calls=%async_computation.20 | async-start | bytes 2654208 | tf_op jit(solution)/shard_map/reduce_scatter | solution.py:334
  922.5 245.1 %reduce-scatter.34.cloned.1.call-start = ((), (), s32[]{:S(2)}) async-start(), calls=%async_computation.21 | async-start | bytes 2654208 | tf_op jit(solution)/shard_map/reduce_scatter | solution.py:335
  932.7 300.6 %reduce-scatter.36.cloned.1.call-start = ((), (), s32[]{:S(2)}) async-start(), calls=%async_computation.22 | async-start | bytes 884736
  940.6 358.3 %reduce-scatter.38.cloned.1.call-start = ((), (), s32[]{:S(2)}) async-start(), calls=%async_computation.23 | async-start | bytes 884736
  948.4 416.2 %reduce-scatter.40.cloned.1.call-start = ((), (), s32[]{:S(2)}) async-start(), calls=%async_computation.24 | async-start | bytes 884736
  1021.2 48.1 %copy-start.4 = (f32[1024,768]{1,0:T(8,128)S(1)}, f32[1024,768]{1,0:T(8,128)}, u32[]{:S(2)}) copy-start(f32[1024,768]{1,0:T(8,128)} %copy-done.3) | copy-start | bytes 9437188
  1021.3 48.1 %copy-start.33 = (f32[1024]{0:T(1024)S(1)}, f32[1024]{0:T(1024)}, u32[]{:S(2)}) copy-start(f32[1024]{0:T(1024)} %copy-done.32) | copy-start | bytes 12292
  1021.3 48.1 %copy-start.37 = (f32[1024]{0:T(1024)S(1)}, f32[1024]{0:T(1024)}, u32[]{:S(2)}) copy-start(f32[1024]{0:T(1024)} %copy-done.36) | copy-start | bytes 12292
  (70 other events, 332.9 us)
Sparse Core Ops, SparseCore 0:
  10.4 49.0 all-gather.8
  268.1 57.7 reduce-scatter.23
  591.0 58.1 reduce-scatter.27
Sparse Core Ops, SparseCore 1:
  270.9 39.8 all-gather.12
  331.6 46.1 all-gather.10
  380.1 41.5 all-gather.14
  431.0 56.7 reduce-scatter.25
  657.8 46.2 all-gather.16
  708.4 61.3 reduce-scatter.43
  898.9 62.6 reduce-scatter.41
  963.9 57.3 reduce-scatter.29
  1025.6 69.4 reduce-scatter.31
  1099.6 68.0 reduce-scatter.33
  1171.8 61.5 reduce-scatter.35
  1237.2 61.6 reduce-scatter.37
  1303.0 61.5 reduce-scatter.39
